TPU v7x, 32 devices: a whole 2x2x4 slice. The times are simulated.
32 devices in a mesh: rows: 8 (over z, y), cls: 4 (over x, core).
Axes of the slice: x: 2, y: 2, z: 4, core: 2. Of those that a mesh axis runs over, the one named last changes fastest.
Arguments:
- features: bfloat16 [6144, 2048], P('rows', 'cls'), may hold values from -32 to 32
- prototypes: bfloat16 [2048, 16384], P('rows', 'cls'), may hold values from -1 to 1
Outputs:
- grad_proto: float32 [2048, 16384], P('rows', 'cls')
All inputs are finite; a program needn't handle non-finite values.
Results may differ from a plain program's by a relative error of at most 0.02.
Values may be sent and summed in bfloat16 or wider, within the bound.
A program may use at most 128 MiB of HBM per device.

v0:
```python
import jax
import jax.numpy as jnp
from jax import lax
from jax.sharding import PartitionSpec as P

ITERS = 3
code_temp = 0.2
loss_temp = 0.3


def local(features, prototypes):
    gathered = lax.all_gather(features, "cls", axis=1, tiled=True)
    local_rows = gathered.shape[0]
    local_classes = prototypes.shape[1]
    balance_ratio = float(local_rows * lax.axis_size("rows")) / float(
        local_classes * lax.axis_size("cls")
    )
    columns = gathered
    scores = jnp.dot(
        columns,
        lax.all_gather(prototypes, "rows", axis=0, tiled=True),
        preferred_element_type=jnp.float32,
    )
    local_top = jnp.max(scores, axis=1)
    row_top = lax.pmax(local_top, "cls")
    shifted = scores - row_top[:, None]
    exp_codes = jnp.exp(shifted / code_temp)
    exp_loss = jnp.exp(shifted / loss_temp)
    sink_total, soft_total = lax.psum(
        (jnp.sum(exp_codes, axis=1), jnp.sum(exp_loss, axis=1)), "cls"
    )
    codes = exp_codes / sink_total[:, None]
    for sweep in range(ITERS):
        col_mass = lax.psum(jnp.sum(codes, axis=0), "rows")
        codes = codes * (balance_ratio / col_mass)[None, :]
        row_mass = lax.psum(jnp.sum(codes, axis=1), "cls")
        codes = codes / row_mass[:, None]
    probs_loss = exp_loss / soft_total[:, None]
    slope = ((probs_loss - codes) / loss_temp).astype(jnp.bfloat16)
    columns = gathered
    return lax.psum_scatter(
        lax.dot_general(
            columns, slope, (((0,), (0,)), ((), ())), preferred_element_type=jnp.float32
        ).astype(jnp.bfloat16),
        "rows",
        scatter_dimension=0,
        tiled=True,
    ).astype(jnp.float32)


def solution(mesh):
    return jax.shard_map(
        local,
        mesh=mesh,
        in_specs=(P("rows", "cls"), P("rows", "cls")),
        out_specs=P("rows", "cls"),
        check_vma=False,
    )
```

profile of v0, /device:TPU:0, one launch (start us, length us, event | category | flops | bytes accessed | tf_op | source)
XLA Modules:
  0.0 786.4 jit_solution(6704144554605490783)
XLA Ops:
  6.5 0.0 all-gather.3.cloned.1.call-start
  6.5 0.7 all-gather.3.cloned.1.call-update
  7.3 0.0 all-gather.5.cloned.1.call-start
  7.3 0.7 all-gather.5.cloned.1.call-update
  8.0 0.0 reduce-scatter.2.cloned.1.call-start
  8.1 32.1 %all-gather.3.cloned.1.call-done = bf16[768,2048]{1,0:T(8,128)(2,1)} async-done(((bf16[768,512]{1,0:T(8,128)(2,1)}), bf16[768,2048]{1,0:T(8,128)(2,1)}) %all-gather.3.cloned.1.call-update) | async-done | bytes 3145744 | tf_op jit(solution)/shard_map/all_gather | solution.py:12
  40.2 229.8 %all-gather.5.cloned.1.call-done = bf16[2048,4096]{1,0:T(8,128)(2,1)} async-done(((bf16[256,4096]{1,0:T(8,128)(2,1)}), bf16[2048,4096]{1,0:T(8,128)(2,1)}) %all-gather.5.cloned.1.call-update) | async-done | bytes 16777232 | tf_op jit(solution)/shard_map/all_gather | solution.py:21
  270.0 20.3 %fusion.8 = (f32[768]{0:T(1024)S(1)}, f32[768,4096]{1,0:T(8,128)}) fusion(bf16[768,2048]{1,0:T(8,128)(2,1)} %all-gather.3.cloned.1.call-done, bf16[2048,4096]{1,0:T(8,128)(2,1)} %all-gather.5.cloned.1.call-done), kind=kOutput, calls=%fused_computation.19 | convolution fusion | flops 12888046592 | bytes 32508928 | tf_op jit(solution)/shard_map/dot_general | solution.py:19
  290.3 6.1 pmax.7
  296.4 7.1 fusion
  303.5 6.1 psum.57
  309.7 11.3 %fusion.6 = (f32[4096]{0:T(1024)S(1)}, f32[768,4096]{1,0:T(8,128)}) fusion(f32[768]{0:T(1024)S(1)} %psum.57, f32[768,4096]{1,0:T(8,128)} %get-tuple-element.14, f32[768]{0:T(1024)S(1)} %pmax.7), kind=kLoop, calls=%fused_computation.18 | loop fusion | flops 12578816 | bytes 25188352 | tf_op jit(solution)/shard_map/reduce_sum | solution.py:34
  320.9 34.6 %psum.58 = f32[4096]{0:T(1024)S(1)} all-reduce(f32[4096]{0:T(1024)S(1)} %get-tuple-element.11), channel_id=1, replica_groups=mesh['rows'=8,'cls'=4] {'rows'}, use_global_device_ids=true, to_apply=%region_7.0 | all-reduce | flops 4096 | bytes 32768 | tf_op jit(solution)/shard_map/psum | solution.py:34
  355.6 5.5 multiply_reduce_fusion.2
  361.1 5.8 psum.59
  366.8 6.4 fusion.4
  373.3 33.2 %psum.60 = f32[4096]{0:T(1024)S(1)} all-reduce(f32[4096]{0:T(1024)S(1)} %fusion.4), channel_id=1, replica_groups=mesh['rows'=8,'cls'=4] {'rows'}, use_global_device_ids=true, to_apply=%region_11.0 | all-reduce | flops 4096 | bytes 32768 | tf_op jit(solution)/shard_map/psum | solution.py:34
  406.5 6.0 multiply_reduce_fusion.1
  412.4 5.8 psum.61
  418.2 11.3 %fusion.5 = (f32[4096]{0:T(1024)S(1)}, f32[768,4096]{1,0:T(8,128)}) fusion(f32[768]{0:T(1024)S(1)} %psum.61, f32[4096]{0:T(1024)S(1)} %broadcast_divide_fusion.1, f32[768]{0:T(1024)S(1)} %psum.59, f32[768,4096]{1,0:T(8,128)} %get-tuple-element.12, f32[4096]{0:T(1024)S(1)} %broadcast_divide_fusion.2), kind=kLoop, calls=%fused_computation.17 | loop fusion | flops 15724544 | bytes 25221120 | tf_op jit(solution)/shard_map/reduce_sum | solution.py:34
  429.5 0.0 copy-start
  429.5 33.2 %psum.62 = f32[4096]{0:T(1024)S(1)} all-reduce(f32[4096]{0:T(1024)S(1)} %get-tuple-element.9), channel_id=1, replica_groups=mesh['rows'=8,'cls'=4] {'rows'}, use_global_device_ids=true, to_apply=%region_15.0 | all-reduce | flops 4096 | bytes 32768 | tf_op jit(solution)/shard_map/psum | solution.py:34
  462.7 5.5 multiply_reduce_fusion
  468.2 5.9 all-reduce
  474.1 0.0 copy-done
  474.1 22.6 %convert_bitcast_fusion = bf16[2048,4096]{0,1:T(8,128)(2,1)} fusion(bf16[768,2048]{1,0:T(8,128)(2,1)S(1)} %copy-done, f32[768,4096]{1,0:T(8,128)} %get-tuple-element.10, f32[768,4096]{1,0:T(8,128)} %get-tuple-element.14, f32[768]{0:T(1024)S(1)} %get-tuple-element.7, f32[4096]{0:T(1024)S(1)} %broadcast_divide_fusion, f32[768]{0:T(1024)S(1)} %get-tuple-element.8, ...), kind=kOutput, calls=%fused_computation | convolution fusion | flops 12918456320 | bytes 45114368 | tf_op jit(solution)/shard_map/dot_general | solution.py:42
  496.7 0.0 reduce-scatter.2.cloned.1.call-update
  496.8 278.8 %reduce-scatter.2.cloned.1.call-done = bf16[256,4096]{0,1:T(8,128)(2,1)} async-done(((bf16[2048,4096]{0,1:T(8,128)(2,1)}), bf16[256,4096]{0,1:T(8,128)(2,1)}) %reduce-scatter.2.cloned.1.call-update) | async-done | bytes 2097168 | tf_op jit(solution)/shard_map/reduce_scatter | solution.py:41
  775.6 4.3 copy.3
  (3 shorter events, 0.0 us)
Async XLA Ops:
  6.5 33.6 %all-gather.3.cloned.1.call-start = ((), (), s32[]{:S(2)}) async-start(), calls=%async_computation.1 | async-start | bytes 3932160 | tf_op jit(solution)/shard_map/all_gather | solution.py:12
  7.3 262.7 %all-gather.5.cloned.1.call-start = ((), (), s32[]{:S(2)}) async-start(), calls=%async_computation.2 | async-start | bytes 18874368 | tf_op jit(solution)/shard_map/all_gather | solution.py:21
  8.0 767.6 %reduce-scatter.2.cloned.1.call-start = ((), (), s32[]{:S(2)}) async-start(), calls=%async_computation.3 | async-start | bytes 18874368 | tf_op jit(solution)/shard_map/reduce_scatter | solution.py:41
  429.5 44.6 %copy-start = (bf16[768,2048]{1,0:T(8,128)(2,1)S(1)}, bf16[768,2048]{1,0:T(8,128)(2,1)}, u32[]{:S(2)}) copy-start(bf16[768,2048]{1,0:T(8,128)(2,1)} %all-gather.3.cloned.1.call-done) | copy-start | bytes 9437188
Sparse Core Ops, SparseCore 0:
  8.9 31.2 all-gather.2
  42.3 227.6 all-gather.4
  496.9 278.6 reduce-scatter.1
where the time goes:
time: 787 us; the launch traced here: 786 us
  waiting for transfers between devices  542 us (69%)
  blocking collectives  131 us (17%)
  other arithmetic  53.1 us (7%)
  matrix products  42.9 us (5%)
  between operations  13.1 us (2%)
    reduce_scatter x1, waiting for transfers between devices, local(): lax.psum_scatter(lax.dot_general(columns, slope, (((0,), (0,)), ((), ()))...  279 us
    all_gather x1, waiting for transfers between devices, local(): lax.all_gather(prototypes, 'rows', axis=0, tiled=True)  230 us
    psum x3, blocking collectives, local(): col_mass = lax.psum(jnp.sum(codes, axis=0), 'rows')  101 us
    all_gather x1, waiting for transfers between devices, local(): gathered = lax.all_gather(features, 'cls', axis=1, tiled=True)  32.1 us
    reduce_sum x3, other arithmetic, local(): col_mass = lax.psum(jnp.sum(codes, axis=0), 'rows')  29 us
    dot_general x1, matrix products, local(): lax.dot_general(columns, slope, (((0,), (0,)), ((), ())), preferred_eleme...  22.6 us
    dot_general x1, matrix products, local(): jnp.dot(columns, lax.all_gather(prototypes, 'rows', axis=0, tiled=True),...  20.3 us
    psum x3, blocking collectives, local(): row_mass = lax.psum(jnp.sum(codes, axis=1), 'cls')  17.4 us
  transfers between devices with their start and end apart: 3, of which 3 were waited for; matrix products, arithmetic and copies ran while one was open for 0% of the time, Pallas kernels for 0%

commit v1 on v0

--- a/solution.py
+++ b/solution.py
@@ -1,15 +1,37 @@
+import functools
 import jax
 import jax.numpy as jnp
 from jax import lax
 from jax.sharding import PartitionSpec as P
+from jax.lax import axis_index, axis_size, ppermute
 
 ITERS = 3
 code_temp = 0.2
 loss_temp = 0.3
 
 
+def find_ports_on(w_in, along_axis):
+    n_dev_all = axis_size(along_axis)
+    shelf = []
+    i0 = 0
+    while i0 < n_dev_all:
+        shelf.append((i0, (i0 + 1) % n_dev_all))
+        i0 += 1
+    b_next = [None] * n_dev_all
+    b_next[n_dev_all - 1] = w_in
+    for j in range(n_dev_all - 2, -1, -1):
+        b_next[j] = ppermute(b_next[j + 1], along_axis, shelf)
+    carry_in = jnp.concatenate(b_next, 1)
+    found_now = axis_index(along_axis)
+    y1 = (found_now + 1) * w_in.shape[1]
+    return jnp.roll(carry_in, y1, 1)
+
+
+settle_paths = functools.partial(find_ports_on, along_axis="cls")
+
+
 def local(features, prototypes):
-    gathered = lax.all_gather(features, "cls", axis=1, tiled=True)
+    gathered = settle_paths(features)
     local_rows = gathered.shape[0]
     local_classes = prototypes.shape[1]
     balance_ratio = float(local_rows * lax.axis_size("rows")) / float(

time: 787 us -> 758 us (0.963)
  waiting for transfers between devices: 542 us -> 502 us
    all_gather x1, waiting for transfers between devices: 230 us -> 188 us  [local(): lax.all_gather(prototypes, 'rows', axis=0, tiled=True)]
    ppermute x0 -> x3, waiting for transfers between devices: none -> 34.6 us  [find_ports_on(): b_next[j] = ppermute(b_next[j + 1], along_axis, shelf)]
    all_gather x1 -> x0, waiting for transfers between devices: 32.1 us -> none  [local(): gathered = lax.all_gather(features, 'cls', axis=1, tiled=True)]
    unnamed x2 -> x9, local copies, waits for them, and re-layouts: 0.01 us -> 8.16 us
  transfers between devices with their start and end apart: 3 -> 5, of which waited for: 3 -> 5; matrix products, arithmetic and copies ran while one was open for 0% -> 1% of each run, Pallas kernels for 0% -> 0%
where the time goes in v1:
time: 758 us; the launch traced here: 757 us
  waiting for transfers between devices  502 us (66%)
  blocking collectives  130 us (17%)
  other arithmetic  57.2 us (8%)
  matrix products  44.7 us (6%)
  between operations  13.4 us (2%)
  local copies, waits for them, and re-layouts  9.14 us (1%)
    reduce_scatter x1, waiting for transfers between devices, local(): lax.psum_scatter(lax.dot_general(columns, slope, (((0,), (0,)), ((), ()))...  278 us
    all_gather x1, waiting for transfers between devices, local(): lax.all_gather(prototypes, 'rows', axis=0, tiled=True)  188 us
    psum x3, blocking collectives, local(): col_mass = lax.psum(jnp.sum(codes, axis=0), 'rows')  101 us
    ppermute x3, waiting for transfers between devices, find_ports_on(): b_next[j] = ppermute(b_next[j + 1], along_axis, shelf)  34.6 us
    reduce_sum x3, other arithmetic, local(): col_mass = lax.psum(jnp.sum(codes, axis=0), 'rows')  29 us
    dot_general x1, matrix products, local(): lax.dot_general(columns, slope, (((0,), (0,)), ((), ())), preferred_eleme...  24.4 us
    dot_general x1, matrix products, local(): jnp.dot(columns, lax.all_gather(prototypes, 'rows', axis=0, tiled=True),...  20.3 us
    psum x3, blocking collectives, local(): row_mass = lax.psum(jnp.sum(codes, axis=1), 'cls')  17.4 us
  transfers between devices with their start and end apart: 5, of which 5 were waited for; matrix products, arithmetic and copies ran while one was open for 1% of the time, Pallas kernels for 0%

profile of v1, /device:TPU:0, one launch (start us, length us, event | category | flops | bytes accessed | tf_op | source)
XLA Modules:
  0.0 757.0 jit_solution(1527703889865508203)
XLA Ops:
  6.5 0.7 all-gather.2.cloned.1.call-update
  7.8 11.8 %collective-permute-done = bf16[768,512]{1,0:T(8,128)(2,1)S(1)} collective-permute-done((bf16[768,512]{1,0:T(8,128)(2,1)}, bf16[768,512]{1,0:T(8,128)(2,1)S(1)}, u32[]{:S(2)}, u32[]{:S(2)}) %collective-permute-start) | collective-permute-done | bytes 786464 | tf_op jit(solution)/shard_map/ppermute | solution.py:23
  19.7 11.4 %collective-permute-done.1 = bf16[768,512]{1,0:T(8,128)(2,1)S(1)} collective-permute-done((bf16[768,512]{1,0:T(8,128)(2,1)S(1)}, bf16[768,512]{1,0:T(8,128)(2,1)S(1)}, u32[]{:S(2)}, u32[]{:S(2)}) %collective-permute-start.1) | collective-permute-done | bytes 786464 | tf_op jit(solution)/shard_map/ppermute | solution.py:23
  31.0 11.4 %collective-permute-done.2 = bf16[768,512]{1,0:T(8,128)(2,1)S(1)} collective-permute-done((bf16[768,512]{1,0:T(8,128)(2,1)S(1)}, bf16[768,512]{1,0:T(8,128)(2,1)S(1)}, u32[]{:S(2)}, u32[]{:S(2)}) %collective-permute-start.2) | collective-permute-done | bytes 786464 | tf_op jit(solution)/shard_map/ppermute | solution.py:23
  42.5 1.0 constant_dynamic-update-slice_fusion.7
  43.4 1.0 constant_dynamic-update-slice_fusion.6
  44.4 1.0 constant_dynamic-update-slice_fusion.5
  45.4 2.1 constant_dynamic-update-slice_fusion.4
  47.6 1.0 constant_dynamic-update-slice_fusion.3
  48.6 1.0 constant_dynamic-update-slice_fusion.2
  49.5 1.1 constant_dynamic-update-slice_fusion.1
  50.6 1.0 constant_dynamic-update-slice_fusion
  51.6 188.2 %all-gather.2.cloned.1.call-done = bf16[2048,4096]{1,0:T(8,128)(2,1)} async-done(((bf16[256,4096]{1,0:T(8,128)(2,1)}), bf16[2048,4096]{1,0:T(8,128)(2,1)}) %all-gather.2.cloned.1.call-update) | async-done | bytes 16777232 | tf_op jit(solution)/shard_map/all_gather | solution.py:43
  239.8 20.3 %fusion.13 = (f32[768]{0:T(1024)S(1)}, f32[768,4096]{1,0:T(8,128)}) fusion(bf16[2048,4096]{1,0:T(8,128)(2,1)} %all-gather.2.cloned.1.call-done, bf16[768,4096]{1,0:T(8,128)(2,1)} %constant_dynamic-update-slice_fusion, s32[]{:T(128)S(6)} %select_n.14), kind=kOutput, calls=%fused_computation.32 | convolution fusion | flops 12888046592 | bytes 32508932 | tf_op jit(solution)/shard_map/dot_general | solution.py:41
  260.1 6.1 pmax.7
  266.3 7.1 fusion
  273.4 6.1 psum.57
  279.5 11.3 %fusion.11 = (f32[4096]{0:T(1024)S(1)}, f32[768,4096]{1,0:T(8,128)}) fusion(f32[768]{0:T(1024)S(1)} %psum.57, f32[768,4096]{1,0:T(8,128)} %get-tuple-element.14, f32[768]{0:T(1024)S(1)} %pmax.7), kind=kLoop, calls=%fused_computation.31 | loop fusion | flops 12578816 | bytes 25188352 | tf_op jit(solution)/shard_map/reduce_sum | solution.py:56
  290.8 34.6 %psum.58 = f32[4096]{0:T(1024)S(1)} all-reduce(f32[4096]{0:T(1024)S(1)} %get-tuple-element.11), channel_id=1, replica_groups=mesh['rows'=8,'cls'=4] {'rows'}, use_global_device_ids=true, to_apply=%region_7.8 | all-reduce | flops 4096 | bytes 32768 | tf_op jit(solution)/shard_map/psum | solution.py:56
  325.5 5.5 multiply_reduce_fusion.2
  330.9 5.8 psum.59
  336.7 6.4 fusion.9
  343.2 33.2 %psum.60 = f32[4096]{0:T(1024)S(1)} all-reduce(f32[4096]{0:T(1024)S(1)} %fusion.9), channel_id=1, replica_groups=mesh['rows'=8,'cls'=4] {'rows'}, use_global_device_ids=true, to_apply=%region_11.12 | all-reduce | flops 4096 | bytes 32768 | tf_op jit(solution)/shard_map/psum | solution.py:56
  376.3 6.0 multiply_reduce_fusion.1
  382.3 5.8 psum.61
  388.1 11.3 %fusion.10 = (f32[4096]{0:T(1024)S(1)}, f32[768,4096]{1,0:T(8,128)}) fusion(f32[768]{0:T(1024)S(1)} %psum.61, f32[4096]{0:T(1024)S(1)} %broadcast_divide_fusion.1, f32[768]{0:T(1024)S(1)} %psum.59, f32[768,4096]{1,0:T(8,128)} %get-tuple-element.12, f32[4096]{0:T(1024)S(1)} %broadcast_divide_fusion.2), kind=kLoop, calls=%fused_computation.30 | loop fusion | flops 15724544 | bytes 25221120 | tf_op jit(solution)/shard_map/reduce_sum | solution.py:56
  399.4 33.0 %psum.62 = f32[4096]{0:T(1024)S(1)} all-reduce(f32[4096]{0:T(1024)S(1)} %get-tuple-element.9), channel_id=1, replica_groups=mesh['rows'=8,'cls'=4] {'rows'}, use_global_device_ids=true, to_apply=%region_15.16 | all-reduce | flops 4096 | bytes 32768 | tf_op jit(solution)/shard_map/psum | solution.py:56
  432.3 5.5 multiply_reduce_fusion
  437.8 5.9 all-reduce
  443.7 24.4 %convolution_convert_fusion = bf16[2048,4096]{1,0:T(8,128)(2,1)} fusion(f32[768,4096]{1,0:T(8,128)} %get-tuple-element.10, f32[768,4096]{1,0:T(8,128)} %get-tuple-element.14, f32[768]{0:T(1024)S(1)} %get-tuple-element.7, f32[4096]{0:T(1024)S(1)} %broadcast_divide_fusion, f32[768]{0:T(1024)S(1)} %get-tuple-element.8, f32[768]{0:T(1024)S(1)} %pmax.7, ...), kind=kOutput, calls=%fused_computation | convolution fusion | flops 12918456320 | bytes 45114372 | tf_op jit(solution)/shard_map/dot_general | solution.py:64
  468.1 277.9 %reduce-scatter.2.cloned.1.call-done = bf16[256,4096]{1,0:T(8,128)(2,1)} async-done(((bf16[2048,4096]{1,0:T(8,128)(2,1)}), bf16[256,4096]{1,0:T(8,128)(2,1)}) %reduce-scatter.2.cloned.1.call-update) | async-done | bytes 2097168 | tf_op jit(solution)/shard_map/reduce_scatter | solution.py:63
  746.0 4.1 convert_element_type.11
  (11 shorter events, 0.6 us)
Async XLA Ops:
  6.5 44.1 %copy-start = (bf16[768,512]{1,0:T(8,128)(2,1)S(1)}, bf16[768,512]{1,0:T(8,128)(2,1)}, u32[]{:S(2)}) copy-start(bf16[768,512]{1,0:T(8,128)(2,1)} %param.2) | copy-start | bytes 2359300
  6.5 233.3 %all-gather.2.cloned.1.call-start = ((), (), s32[]{:S(2)}) async-start(), calls=%async_computation.1 | async-start | bytes 18874368 | tf_op jit(solution)/shard_map/all_gather | solution.py:43
  7.3 738.8 %reduce-scatter.2.cloned.1.call-start = ((), (), s32[]{:S(2)}) async-start(), calls=%async_computation.2 | async-start | bytes 18874368 | tf_op jit(solution)/shard_map/reduce_scatter | solution.py:63
  7.3 12.3 %collective-permute-start = (bf16[768,512]{1,0:T(8,128)(2,1)}, bf16[768,512]{1,0:T(8,128)(2,1)S(1)}, u32[]{:S(2)}, u32[]{:S(2)}) collective-permute-start(bf16[768,512]{1,0:T(8,128)(2,1)} %param.2), channel_id=1, source_target_pairs={{0,1},{1,2},{2,3},{3,0},{4,5},{5,6},{6,7},{7,4},{8,9},{9,10},{10,1... | collective-permute-start | bytes 2359304 | tf_op jit(solution)/shard_map/ppermute | solution.py:23
  19.6 11.4 %collective-permute-start.1 = (bf16[768,512]{1,0:T(8,128)(2,1)S(1)}, bf16[768,512]{1,0:T(8,128)(2,1)S(1)}, u32[]{:S(2)}, u32[]{:S(2)}) collective-permute-start(bf16[768,512]{1,0:T(8,128)(2,1)S(1)} %collective-permute-done), channel_id=1, source_target_pairs={{0,1},{1,2},{2,3},{3,0},{4,5},{5,6},{6,7},{7,4},{8,9},{9,10},{10,1... | collective-permute-start | bytes 2359304 | tf_op jit(solution)/shard_map/ppermute | solution.py:23
  31.0 11.4 %collective-permute-start.2 = (bf16[768,512]{1,0:T(8,128)(2,1)S(1)}, bf16[768,512]{1,0:T(8,128)(2,1)S(1)}, u32[]{:S(2)}, u32[]{:S(2)}) collective-permute-start(bf16[768,512]{1,0:T(8,128)(2,1)S(1)} %collective-permute-done.1), channel_id=1, source_target_pairs={{0,1},{1,2},{2,3},{3,0},{4,5},{5,6},{6,7},{7,4},{8,9},{9,10},{10,1... | collective-permute-start | bytes 2359304 | tf_op jit(solution)/shard_map/ppermute | solution.py:23
Sparse Core Ops, SparseCore 0:
  9.5 230.3 all-gather.1
  468.2 277.7 reduce-scatter.1
